TPU v7x, 32 devices: a whole 2x2x4 slice. The times are simulated.
32 devices in a mesh: dp: 2 (over x), space: 16 (over z, y, core).
Axes of the slice: x: 2, y: 2, z: 4, core: 2. Of those that a mesh axis runs over, the one named last changes fastest.
Arguments:
- stash: bfloat16 [16, 16, 4, 8640], P('space', None, 'dp'), may hold values from -5 to 5
- piece_map: int32 [16, 16], P(None, 'space'), may hold values from 0 to 15, as said below
- gain_one: float32 [768], replicated, may hold values from 0.5 to 1.5
- spec_one: float32 [2, 8, 96, 96], replicated, may hold values from -0.4375 to 0.4375
- bias_one: float32 [2, 768], replicated, may hold values from -3 to 3
- spec_two: float32 [2, 8, 96, 96], replicated, may hold values from -0.4375 to 0.4375
- bias_two: float32 [2, 768], replicated, may hold values from -0.6 to 0.6
- gain_two: float32 [768], replicated, may hold values from 0.5 to 1.5
- fc_one: bfloat16 [768, 3072], replicated, may hold values from -0.21875 to 0.21875
- bias_fc: float32 [3072], replicated, may hold values from -3 to 3
- fc_two: bfloat16 [3072, 768], replicated, may hold values from -0.109375 to 0.109375
- cotangent: bfloat16 [4, 16, 180, 768], P('dp', 'space'), may hold values from -6 to 6
Outputs:
- grad_input: float32 [4, 16, 180, 768], P('dp', 'space')
- grad_fc_one: float32 [768, 3072], P(None, ('dp', 'space'))
- grad_fc_two: float32 [3072, 768], P(('dp', 'space'))
- grad_bias_fc: float32 [3072], replicated
- grad_bias_out: float32 [768], replicated
- grad_gain_one: float32 [768], replicated
- grad_gain_two: float32 [768], replicated
- grad_spec_one: float32 [2, 8, 96, 96], replicated
- grad_bias_one: float32 [2, 768], replicated
- grad_spec_two: float32 [2, 8, 96, 96], replicated
- grad_bias_two: float32 [2, 768], replicated
Inputs may be any that keep to these rules, and one draw needn't show every extreme that they name: `piece_map`: each column holds every number from 0 to 15 once.
All inputs are finite; a program needn't handle non-finite values.
Results may differ from a plain program's by a relative error of at most 0.0046.
Values may be sent and summed in bfloat16 or wider, within the bound.
A program may use at most 128 MiB of HBM per device.

v0:
```python
import math
import jax
import jax.numpy as jnp
from jax import lax
from jax.sharding import PartitionSpec as P

KW = 64
epsilon = 1e-05
highest = lax.Precision.HIGHEST


def layer_norm(values, gain_vector):
    centred = values - jnp.mean(values, axis=-1, keepdims=True)
    spread = jnp.mean(centred * centred, axis=-1, keepdims=True)
    return centred * lax.rsqrt(spread + epsilon) * gain_vector


def smooth_gate(values):
    return jax.nn.gelu(values, approximate=True)


def block_mix(real_part, imag_part, weights, biases):
    blocks = weights.shape[1]
    width_block = weights.shape[2]
    leading = real_part.shape[:-1]
    real_blocks = real_part.reshape(leading + (blocks, width_block))
    imag_blocks = imag_part.reshape(leading + (blocks, width_block))
    bias_real = biases[0].reshape(blocks, width_block)
    bias_imag = biases[1].reshape(blocks, width_block)
    new_real = (
        jnp.einsum("...ni,nio->...no", real_blocks, weights[0], precision=highest)
        - jnp.einsum("...ni,nio->...no", imag_blocks, weights[1], precision=highest)
        + bias_real
    )
    new_imag = (
        jnp.einsum("...ni,nio->...no", real_blocks, weights[1], precision=highest)
        + jnp.einsum("...ni,nio->...no", imag_blocks, weights[0], precision=highest)
        + bias_imag
    )
    return (
        new_real.reshape(leading + (blocks * width_block,)),
        new_imag.reshape(leading + (blocks * width_block,)),
    )


def spectral_mlp(spec_real, spec_imag, spec_one, bias_one, spec_two, bias_two):
    inner_real, inner_imag = block_mix(spec_real, spec_imag, spec_one, bias_one)
    return block_mix(smooth_gate(inner_real), smooth_gate(inner_imag), spec_two, bias_two)


def wave_tables(length, total_modes):
    positions = jnp.arange(length, dtype=jnp.int32)
    frequency = jnp.arange(total_modes, dtype=jnp.int32)
    phases = positions[:, None] * frequency[None, :] % length
    angles = phases.astype(jnp.float32) * (2.0 * math.pi / length)
    factor = 1.0 / math.sqrt(length)
    return (jnp.cos(angles) * factor, jnp.sin(angles) * factor)


def meridian_apply(table, field):
    return jnp.einsum("hk,bhmd->bkmd", table, field, precision=highest)


def meridian_forward(real_part, imag_part, merid_cos, merid_sin):
    new_real = meridian_apply(merid_cos, real_part) + meridian_apply(merid_sin, imag_part)
    new_imag = meridian_apply(merid_cos, imag_part) - meridian_apply(merid_sin, real_part)
    return (new_real, new_imag)


def meridian_inverse(real_part, imag_part, merid_cos, merid_sin):
    new_real = meridian_apply(merid_cos, real_part) - meridian_apply(merid_sin, imag_part)
    new_imag = meridian_apply(merid_cos, imag_part) + meridian_apply(merid_sin, real_part)
    return (new_real, new_imag)


def zonal_project(field, table):
    return jnp.einsum("brwd,wk->brkd", field, table, precision=highest)


def zonal_expand(field, table):
    return jnp.einsum("brkd,wk->brwd", field, table, precision=highest)


def local(
    stash,
    piece_map,
    gain_one,
    spec_one,
    bias_one,
    spec_two,
    bias_two,
    gain_two,
    fc_one,
    bias_fc,
    fc_two,
    cotangent,
):
    samples, lat_rows, lon_cells, model_width = cotangent.shape
    space_ranks = lax.axis_size("space")
    lat_total = lat_rows * space_ranks
    tokens = samples * lat_rows * lon_cells
    arrived = lax.all_to_all(stash, "space", split_axis=1, concat_axis=0, tiled=True)
    ordering = jnp.argsort(piece_map[:, 0])
    placed = jnp.take(arrived[:, 0], ordering, axis=0)
    inputs = jnp.transpose(placed, (1, 0, 2)).reshape(samples, lat_rows, lon_cells, model_width)
    base_field = inputs.astype(jnp.float32)
    zonal_cos, zonal_sin = wave_tables(lon_cells, KW)
    doubling = jnp.where(jnp.arange(KW) == 0, 1.0, 2.0).astype(jnp.float32)
    back_cos = zonal_cos * doubling
    back_sin = zonal_sin * doubling
    merid_cos, merid_sin = wave_tables(lat_total, lat_total)
    normed, pull_one = jax.vjp(layer_norm, base_field, gain_one)
    zonal_real = zonal_project(normed, zonal_cos)
    zonal_imag = -zonal_project(normed, zonal_sin)
    modes_real, modes_imag = (
        lax.all_to_all(zonal_real, "space", split_axis=2, concat_axis=1, tiled=True),
        lax.all_to_all(zonal_imag, "space", split_axis=2, concat_axis=1, tiled=True),
    )
    spec_real, spec_imag = meridian_forward(modes_real, modes_imag, merid_cos, merid_sin)
    mixed_spec, pull_mix = jax.vjp(
        spectral_mlp, spec_real, spec_imag, spec_one, bias_one, spec_two, bias_two
    )
    back_real, back_imag = meridian_inverse(mixed_spec[0], mixed_spec[1], merid_cos, merid_sin)
    rows_real, rows_imag = (
        lax.all_to_all(back_real, "space", split_axis=1, concat_axis=2, tiled=True),
        lax.all_to_all(back_imag, "space", split_axis=1, concat_axis=2, tiled=True),
    )
    spatial = zonal_expand(rows_real, back_cos) - zonal_expand(rows_imag, back_sin)
    mixed_field = base_field + normed + spatial
    normed_two, pull_two = jax.vjp(layer_norm, mixed_field, gain_two)
    normed_flat = normed_two.astype(jnp.bfloat16).reshape(tokens, model_width)
    hidden_pre = jnp.dot(normed_flat, fc_one, preferred_element_type=jnp.float32) + bias_fc
    active, pull_gate = jax.vjp(smooth_gate, hidden_pre)
    active_flat = active.astype(jnp.bfloat16)
    upstream = cotangent.reshape(tokens, model_width)
    grad_active = jnp.einsum("td,fd->tf", upstream, fc_two, preferred_element_type=jnp.float32)
    grad_hidden = pull_gate(grad_active)[0]
    grad_hidden_flat = grad_hidden.astype(jnp.bfloat16)
    grad_normed_two = jnp.einsum(
        "tf,df->td", grad_hidden_flat, fc_one, preferred_element_type=jnp.float32
    )
    term_one = jnp.einsum(
        "td,tf->df", normed_flat, grad_hidden_flat, preferred_element_type=jnp.float32
    )
    term_two = jnp.einsum("td,tf->df", upstream, active_flat, preferred_element_type=jnp.float32)
    grad_mixed_norm, grad_gain_two = pull_two(grad_normed_two.reshape(mixed_field.shape))
    grad_mixed = cotangent.astype(jnp.float32) + grad_mixed_norm
    grad_back_real = zonal_project(grad_mixed, back_cos)
    grad_back_imag = -zonal_project(grad_mixed, back_sin)
    grad_modes_real, grad_modes_imag = (
        lax.all_to_all(grad_back_real, "space", split_axis=2, concat_axis=1, tiled=True),
        lax.all_to_all(grad_back_imag, "space", split_axis=2, concat_axis=1, tiled=True),
    )
    grad_out_real, grad_out_imag = meridian_forward(
        grad_modes_real, grad_modes_imag, merid_cos, merid_sin
    )
    pulled = pull_mix((grad_out_real, grad_out_imag))
    grad_merid_real, grad_merid_imag = meridian_inverse(pulled[0], pulled[1], merid_cos, merid_sin)
    grad_rows_real, grad_rows_imag = (
        lax.all_to_all(grad_merid_real, "space", split_axis=1, concat_axis=2, tiled=True),
        lax.all_to_all(grad_merid_imag, "space", split_axis=1, concat_axis=2, tiled=True),
    )
    grad_normed = (
        grad_mixed
        + zonal_expand(grad_rows_real, zonal_cos)
        - zonal_expand(grad_rows_imag, zonal_sin)
    )
    grad_base, grad_gain_one = pull_one(grad_normed)
    grad_input = grad_mixed + grad_base
    bias_sum = jnp.sum(grad_hidden, axis=0)
    out_sum = jnp.sum(cotangent, axis=(0, 1, 2), dtype=jnp.float32)
    totals = lax.psum(
        (
            grad_gain_one,
            grad_gain_two,
            pulled[2],
            pulled[3],
            pulled[4],
            pulled[5],
            bias_sum,
            out_sum,
        ),
        ("dp", "space"),
    )
    paired = (
        lax.psum_scatter(term_one, "dp", scatter_dimension=1, tiled=True),
        lax.psum_scatter(term_two, "dp", scatter_dimension=1, tiled=True),
    )
    summed = (
        lax.psum_scatter(paired[0], "space", scatter_dimension=1, tiled=True),
        lax.psum_scatter(paired[1], "space", scatter_dimension=1, tiled=True),
    )
    grad_scale = 1.0 / math.sqrt(samples * lax.axis_size("dp") * lat_total * lon_cells)
    return (
        grad_input,
        summed[0] * grad_scale,
        (summed[1] * grad_scale).T,
        totals[6] * grad_scale,
        totals[7] * grad_scale,
        totals[0] * grad_scale,
        totals[1] * grad_scale,
        totals[2] * grad_scale,
        totals[3] * grad_scale,
        totals[4] * grad_scale,
        totals[5] * grad_scale,
    )


def solution(mesh):
    placed = (
        P("space", None, "dp", None),
        P(None, "space"),
        P(),
        P(),
        P(),
        P(),
        P(),
        P(),
        P(),
        P(),
        P(),
        P("dp", "space", None, None),
    )
    return jax.shard_map(
        local,
        mesh=mesh,
        in_specs=placed,
        out_specs=(
            P("dp", "space", None, None),
            P(None, ("dp", "space")),
            P(("dp", "space"), None),
            P(),
            P(),
            P(),
            P(),
            P(),
            P(),
            P(),
            P(),
        ),
        check_vma=False,
    )
```

profile of v0, /device:TPU:0, one launch (start us, length us, event | category | flops | bytes accessed | tf_op | source)
XLA Modules:
  0.0 540.8 jit_solution(15111530025571040540)
XLA Ops:
  8.0 7.4 %all-to-all-start = ((bf16[1,16,2,8640]{3,2,0,1:T(2,128)(2,1)}), bf16[1,16,2,8640]{3,2,0,1:T(2,128)(2,1)S(1)}, u32[]{:S(2)}, u32[]{:S(2)}) async-start(bf16[1,16,2,8640]{3,2,0,1:T(2,128)(2,1)} %bitcast.441), calls=%async_computation | async-start | bytes 1114112 | tf_op jit(solution)/shard_map/all_to_all | solution.py:102
  15.5 1.9 sort.17
  17.4 12.9 %all-to-all-done = bf16[1,16,2,8640]{3,2,0,1:T(2,128)(2,1)S(1)} async-done(((bf16[1,16,2,8640]{3,2,0,1:T(2,128)(2,1)}), bf16[1,16,2,8640]{3,2,0,1:T(2,128)(2,1)S(1)}, u32[]{:S(2)}, u32[]{:S(2)}) %all-to-all-start) | async-done | bytes 552992 | tf_op jit(solution)/shard_map/all_to_all | solution.py:102
  30.2 1.7 gather_fusion
  34.9 1.2 convolution_bitcast_fusion.4
  37.2 4.3 all-to-all-start.1
  41.6 1.3 fusion.29
  43.9 9.8 %all-to-all-done.1 = f32[2,1,64,768]{3,0,1,2:T(2,128)S(1)} async-done(((f32[2,1,64,768]{3,0,1,2:T(2,128)}), f32[2,1,64,768]{3,0,1,2:T(2,128)S(1)}, u32[]{:S(2)}, u32[]{:S(2)}) %all-to-all-start.1) | async-done | bytes 393248 | tf_op jit(solution)/shard_map/all_to_all | solution.py:116
  53.7 4.0 all-to-all-start.2
  58.1 1.3 fusion.143
  59.5 10.4 %all-to-all-done.2 = f32[2,1,64,768]{3,0,1,2:T(2,128)S(1)} async-done(((f32[2,1,64,768]{3,0,1,2:T(2,128)}), f32[2,1,64,768]{3,0,1,2:T(2,128)S(1)}, u32[]{:S(2)}, u32[]{:S(2)}) %all-to-all-start.2) | async-done | bytes 393248 | tf_op jit(solution)/shard_map/all_to_all | solution.py:117
  69.9 1.3 fusion.139
  71.2 1.6 fusion.28
  73.8 1.5 fusion.106
  75.3 1.3 fusion.27
  76.6 1.3 reshape.375
  80.1 1.6 fusion.111
  84.3 1.8 fusion.19
  88.7 3.7 all-to-all-start.3
  95.5 9.1 %all-to-all-done.3 = f32[2,16,4,768]{3,2,0,1:T(4,128)S(1)} async-done(((f32[2,16,4,768]{3,2,0,1:T(4,128)}), f32[2,16,4,768]{3,2,0,1:T(4,128)S(1)}, u32[]{:S(2)}, u32[]{:S(2)}) %all-to-all-start.3) | async-done | bytes 393248 | tf_op jit(solution)/shard_map/all_to_all | solution.py:125
  104.5 3.6 all-to-all-start.4
  108.2 6.3 %fusion.368 = f32[360,3072]{1,0:T(8,128)} fusion(bf16[360,768]{1,0:T(8,128)(2,1)S(1)} %copy-done.24, bf16[3072,768]{1,0:T(8,128)(2,1)} %param.22), kind=kOutput, calls=%fused_computation.459 | convolution fusion | flops 1698693120 | bytes 9695232 | tf_op jit(solution)/shard_map/td,fd->tf/dot_general | solution.py:136
  114.7 1.3 fusion.131
  116.1 4.2 all-to-all-done.4
  120.4 1.6 fusion.365
  123.4 9.3 %fusion.363 = (f32[3072]{0:T(1024)S(1)}, bf16[360,3072]{1,0:T(8,128)(2,1)S(1)}, f32[360,3072]{1,0:T(8,128)}) fusion(f32[360,3072]{1,0:T(8,128)} %fusion.368, f32[3072]{0:T(1024)S(1)} %copy-done.30, bf16[360,768]{1,0:T(8,128)(2,1)S(1)} %reshape.380, bf16[768,3072]{1,0:T(8,128)(2,1)} %param.20), kind=kOutput, calls=%fused_computation.455 | convolution fusion | flops 1723020288 | bytes 16355328 | tf_op jit(solution)/shard_map/dot_general | solution.py:132
  132.8 1.4 copy-done.17
  134.2 5.1 fusion.32
  140.4 8.9 %convolution_bitcast_fusion = f32[768,3072]{0,1:T(8,128)} fusion(bf16[360,768]{1,0:T(8,128)(2,1)S(1)} %copy-done.25, f32[360,3072]{1,0:T(8,128)} %get-tuple-element.83), kind=kOutput, calls=%fused_computation.3 | convolution fusion | flops 1708646400 | bytes 14413824 | tf_op jit(solution)/shard_map/td,tf->df/dot_general | solution.py:145
  149.3 6.0 %fusion.34 = f32[360,768]{1,0:T(8,128)} fusion(bf16[768,3072]{1,0:T(8,128)(2,1)} %param.20, bf16[360,3072]{1,0:T(8,128)(2,1)} %copy-done.17), kind=kOutput, calls=%fused_computation.86 | convolution fusion | flops 1698693120 | bytes 8036352 | tf_op jit(solution)/shard_map/tf,df->td/dot_general | solution.py:139
  155.2 1.4 reshape.381
  158.6 1.7 convert_reduce_fusion
  162.5 3.7 all-to-all-start.6
  168.4 10.0 %all-to-all-done.6 = f32[2,1,64,768]{3,0,1,2:T(2,128)S(1)} async-done(((f32[2,1,64,768]{3,0,1,2:T(2,128)}), f32[2,1,64,768]{3,0,1,2:T(2,128)S(1)}, u32[]{:S(2)}, u32[]{:S(2)}) %all-to-all-start.6) | async-done | bytes 393248 | tf_op jit(solution)/shard_map/all_to_all | solution.py:151
  178.4 3.6 all-to-all-start.5
  182.4 1.3 fusion.133
  183.7 10.3 %all-to-all-done.5 = f32[2,1,64,768]{3,0,1,2:T(2,128)S(1)} async-done(((f32[2,1,64,768]{3,0,1,2:T(2,128)}), f32[2,1,64,768]{3,0,1,2:T(2,128)S(1)}, u32[]{:S(2)}, u32[]{:S(2)}) %all-to-all-start.5) | async-done | bytes 393248 | tf_op jit(solution)/shard_map/all_to_all | solution.py:152
  194.1 1.6 fusion.366
  197.3 1.3 fusion.367
  198.7 1.3 reshape.383
  200.0 2.0 fusion.87
  202.1 1.2 fusion.61
  211.0 1.2 convolution_bitcast_fusion.6
  216.7 33.6 %reduce-scatter.9.cloned.1.call-done = f32[768,1536]{1,0:T(8,128)} async-done(((f32[768,3072]{1,0:T(8,128)}), f32[768,1536]{1,0:T(8,128)}) %reduce-scatter.9.cloned.1.call-update) | async-done | bytes 4718608 | tf_op jit(solution)/shard_map/reduce_scatter | solution.py:186
  250.3 6.1 %copy.208 = f32[768,1536]{0,1:T(8,128)} copy(f32[768,1536]{1,0:T(8,128)} %reduce-scatter.9.cloned.1.call-done) | data formatting | bytes 9437184
  256.5 108.2 %reduce-scatter.11.cloned.1.call-done = f32[768,1536]{0,1:T(8,128)} async-done(((f32[768,3072]{0,1:T(8,128)}), f32[768,1536]{0,1:T(8,128)}) %reduce-scatter.11.cloned.1.call-update) | async-done | bytes 4718608 | tf_op jit(solution)/shard_map/reduce_scatter | solution.py:187
  364.7 1.1 copy-done.6
  365.9 1.9 fusion.124
  368.6 1.1 copy.171
  369.8 1.2 reshape.385
  371.0 1.9 fusion.118
  374.9 1.3 reshape.386
  378.2 5.6 %all-to-all-start.8 = ((f32[2,16,4,768]{3,2,0,1:T(4,128)}), f32[2,16,4,768]{3,2,0,1:T(4,128)S(1)}, u32[]{:S(2)}, u32[]{:S(2)}) async-start(f32[2,16,4,768]{3,2,0,1:T(4,128)} %copy.176), calls=%async_computation.8 | async-start | bytes 786432 | tf_op jit(solution)/shard_map/all_to_all | solution.py:161
  385.9 10.2 %all-to-all-done.8 = f32[2,16,4,768]{3,2,0,1:T(4,128)S(1)} async-done(((f32[2,16,4,768]{3,2,0,1:T(4,128)}), f32[2,16,4,768]{3,2,0,1:T(4,128)S(1)}, u32[]{:S(2)}, u32[]{:S(2)}) %all-to-all-start.8) | async-done | bytes 393248 | tf_op jit(solution)/shard_map/all_to_all | solution.py:161
  396.2 4.0 all-to-all-start.7
  400.4 43.3 %all-reduce.16.cloned.1.call-done = (f32[2,8,96,96]{3,2,1,0:T(8,128)}, f32[2,8,96,96]{3,2,1,0:T(8,128)}) async-done(((f32[2,8,96,96]{3,2,1,0:T(8,128)}, f32[2,8,96,96]{3,2,1,0:T(8,128)}), (f32[2,8,96,96]{3,2,1,0:T(8,128)}, f32[2,8,96,96]{3,2,1,0:T(8,128)})) %all-reduce.16.cloned.1.call-update) | async-done | bytes 1179664 | tf_op jit(solution)/shard_map/psum | solution.py:172
  443.7 2.7 broadcast_multiply_fusion
  446.8 1.3 convolution_bitcast_fusion.1
  448.2 1.7 multiply_reduce_fusion.2
  450.9 2.1 copy.188
  453.0 41.9 %all-reduce.12 = (f32[3072]{0:T(1024)S(1)}, f32[768]{0:T(1024)S(1)}, f32[768]{0:T(1024)S(1)}, f32[768]{0:T(1024)S(1)}, f32[2,768]{1,0:T(2,128)S(1)}, /*index=5*/f32[2,768]{1,0:T(2,128)S(1)}) all-reduce(f32[3072]{0:T(1024)S(1)} %get-tuple-element.73, ...), channel_id=1, replica_groups=mesh['dp'=2,'space'=16] {'dp','space'}, use_global_device_ids=true, to_apply=%region_14.15 | all-reduce | flops 8448 | bytes 67584 | tf_op jit(solution)/shard_map/psum | solution.py:172
  497.4 1.1 copy.209
  499.4 32.0 %reduce-scatter.15.cloned.1.call-done = f32[96,768]{1,0:T(8,128)} async-done(((f32[1536,768]{1,0:T(8,128)}), f32[96,768]{1,0:T(8,128)}) %reduce-scatter.15.cloned.1.call-update) | async-done | bytes 294928
  531.4 1.1 copy.211
  (170 shorter events, 52.8 us)
Async XLA Ops:
  8.0 22.2 %all-to-all-start = ((bf16[1,16,2,8640]{3,2,0,1:T(2,128)(2,1)}), bf16[1,16,2,8640]{3,2,0,1:T(2,128)(2,1)S(1)}, u32[]{:S(2)}, u32[]{:S(2)}) async-start(bf16[1,16,2,8640]{3,2,0,1:T(2,128)(2,1)} %bitcast.441), calls=%async_computation | async-start | bytes 1114112 | tf_op jit(solution)/shard_map/all_to_all | solution.py:102
  34.3 0.7 copy-start.26
  37.2 16.5 %all-to-all-start.1 = ((f32[2,1,64,768]{3,0,1,2:T(2,128)}), f32[2,1,64,768]{3,0,1,2:T(2,128)S(1)}, u32[]{:S(2)}, u32[]{:S(2)}) async-start(f32[2,1,64,768]{3,0,1,2:T(2,128)} %copy.140), calls=%async_computation.1 | async-start | bytes 786432 | tf_op jit(solution)/shard_map/all_to_all | solution.py:116
  42.8 14.9 %copy-start.28 = (f32[2,768]{1,0:T(2,128)S(1)}, f32[2,768]{1,0:T(2,128)}, u32[]{:S(2)}) copy-start(f32[2,768]{1,0:T(2,128)} %param.16) | copy-start | bytes 18436
  42.8 15.1 %copy-start.29 = (f32[2,768]{1,0:T(2,128)S(1)}, f32[2,768]{1,0:T(2,128)}, u32[]{:S(2)}) copy-start(f32[2,768]{1,0:T(2,128)} %param.18) | copy-start | bytes 18436
  53.7 16.1 %all-to-all-start.2 = ((f32[2,1,64,768]{3,0,1,2:T(2,128)}), f32[2,1,64,768]{3,0,1,2:T(2,128)S(1)}, u32[]{:S(2)}, u32[]{:S(2)}) async-start(f32[2,1,64,768]{3,0,1,2:T(2,128)} %copy.142), calls=%async_computation.2 | async-start | bytes 786432 | tf_op jit(solution)/shard_map/all_to_all | solution.py:117
  71.2 1.9 copy-start.5
  73.2 2.1 copy-start.1
  73.2 2.1 copy-start.23
  76.6 1.3 copy-start.22
  78.0 3.7 copy-start.3
  78.0 1.3 copy-start.14
  79.3 2.4 copy-start.20
  82.3 1.3 copy-start.7
  83.2 1.1 copy-start.15
  87.1 5.3 copy-start.18
  88.7 15.8 %all-to-all-start.3 = ((f32[2,16,4,768]{3,2,0,1:T(4,128)}), f32[2,16,4,768]{3,2,0,1:T(4,128)S(1)}, u32[]{:S(2)}, u32[]{:S(2)}) async-start(f32[2,16,4,768]{3,2,0,1:T(4,128)} %copy.152), calls=%async_computation.3 | async-start | bytes 786432 | tf_op jit(solution)/shard_map/all_to_all | solution.py:125
  94.4 13.7 %copy-start.24 = (bf16[360,768]{1,0:T(8,128)(2,1)S(1)}, bf16[360,768]{1,0:T(8,128)(2,1)}, u32[]{:S(2)}) copy-start(bf16[360,768]{1,0:T(8,128)(2,1)} %reshape.373) | copy-start | bytes 1658884
  104.5 15.7 %all-to-all-start.4 = ((f32[2,16,4,768]{3,2,0,1:T(4,128)}), f32[2,16,4,768]{3,2,0,1:T(4,128)S(1)}, u32[]{:S(2)}, u32[]{:S(2)}) async-start(f32[2,16,4,768]{3,2,0,1:T(4,128)} %copy.155), calls=%async_computation.4 | async-start | bytes 786432 | tf_op jit(solution)/shard_map/all_to_all | solution.py:126
  108.1 142.2 %reduce-scatter.9.cloned.1.call-start = ((), (), s32[]{:S(2)}) async-start(), calls=%async_computation.13 | async-start | bytes 14155776 | tf_op jit(solution)/shard_map/reduce_scatter | solution.py:186
  122.0 0.7 copy-start.27
  122.7 0.7 copy-start.30
  132.8 1.5 copy-start.17
  139.3 1.1 copy-start.25
  139.4 225.4 %reduce-scatter.11.cloned.1.call-start = ((), (), s32[]{:S(2)}) async-start(), calls=%async_computation.14 | async-start | bytes 14155776 | tf_op jit(solution)/shard_map/reduce_scatter | solution.py:187
  156.6 1.0 copy-start
  157.6 1.1 copy-start.19
  162.5 15.9 %all-to-all-start.6 = ((f32[2,1,64,768]{3,0,1,2:T(2,128)}), f32[2,1,64,768]{3,0,1,2:T(2,128)S(1)}, u32[]{:S(2)}, u32[]{:S(2)}) async-start(f32[2,1,64,768]{3,0,1,2:T(2,128)} %copy.160), calls=%async_computation.6 | async-start | bytes 786432 | tf_op jit(solution)/shard_map/all_to_all | solution.py:151
  178.4 15.7 %all-to-all-start.5 = ((f32[2,1,64,768]{3,0,1,2:T(2,128)}), f32[2,1,64,768]{3,0,1,2:T(2,128)S(1)}, u32[]{:S(2)}, u32[]{:S(2)}) async-start(f32[2,1,64,768]{3,0,1,2:T(2,128)} %copy.158), calls=%async_computation.5 | async-start | bytes 786432 | tf_op jit(solution)/shard_map/all_to_all | solution.py:152
  181.9 261.8 %all-reduce.16.cloned.1.call-start = ((), (), s32[]{:S(2)}) async-start(), calls=%async_computation.17 | async-start | bytes 3145728 | tf_op jit(solution)/shard_map/psum | solution.py:172
  198.7 3.4 copy-start.8
  200.0 2.1 copy-start.13
  200.0 2.1 copy-start.16
  202.1 1.2 copy-start.2
  203.3 2.3 copy-start.9
  203.3 1.2 copy-start.4
  204.5 1.9 copy-start.21
  207.5 2.1 copy-start.10
  216.7 280.7 %reduce-scatter.13.cloned.1.call-start = ((), (), s32[]{:S(2)}) async-start(), calls=%async_computation.15 | async-start | bytes 5013504
  256.4 275.0 %reduce-scatter.15.cloned.1.call-start = ((), (), s32[]{:S(2)}) async-start(), calls=%async_computation.16 | async-start | bytes 5013504
  364.7 1.1 copy-start.6
  365.9 1.9 copy-start.11
  371.0 1.9 copy-start.12
  378.2 17.9 %all-to-all-start.8 = ((f32[2,16,4,768]{3,2,0,1:T(4,128)}), f32[2,16,4,768]{3,2,0,1:T(4,128)S(1)}, u32[]{:S(2)}, u32[]{:S(2)}) async-start(f32[2,16,4,768]{3,2,0,1:T(4,128)} %copy.176), calls=%async_computation.8 | async-start | bytes 786432 | tf_op jit(solution)/shard_map/all_to_all | solution.py:161
  396.2 50.4 %all-to-all-start.7 = ((f32[2,16,4,768]{3,2,0,1:T(4,128)}), f32[2,16,4,768]{3,2,0,1:T(4,128)S(1)}, u32[]{:S(2)}, u32[]{:S(2)}) async-start(f32[2,16,4,768]{3,2,0,1:T(4,128)} %copy.173), calls=%async_computation.7 | async-start | bytes 786432 | tf_op jit(solution)/shard_map/all_to_all | solution.py:160
Sparse Core Ops, SparseCore 0:
  139.5 110.7 reduce-scatter.8
  252.6 112.1 reduce-scatter.10
  368.6 83.4 reduce-scatter.12
  455.8 75.5 reduce-scatter.14
Sparse Core Ops, SparseCore 1:
  216.7 226.9 all-reduce.15
where the time goes:
time: 549 us; the launch traced here: 541 us
  waiting for transfers between devices  294 us (54%)
  matrix products  88.4 us (16%)
  local copies, waits for them, and re-layouts  44.3 us (8%)
  blocking collectives  41.9 us (8%)
  starting transfers between devices  40.8 us (7%)
  between operations  16.4 us (3%)
  other arithmetic  14.9 us (3%)
    reduce_scatter x1, waiting for transfers between devices, local(): lax.psum_scatter(term_two, 'dp', scatter_dimension=1, tiled=True)  108 us
    psum x1, waiting for transfers between devices, local(): lax.psum((grad_gain_one, grad_gain_two, pulled[2], pulled[3], pulled[4],...  43.3 us
    psum x1, blocking collectives, local(): lax.psum((grad_gain_one, grad_gain_two, pulled[2], pulled[3], pulled[4],...  41.9 us
    reduce_scatter x1, waiting for transfers between devices, local(): lax.psum_scatter(term_one, 'dp', scatter_dimension=1, tiled=True)  33.6 us
    unnamed x7, waiting for transfers between devices  32.1 us
    unnamed x69, local copies, waits for them, and re-layouts  19.4 us
    dot_general x16, matrix products, meridian_apply(): return jnp.einsum('hk,bhmd->bkmd', table, field, precision=highest)  14.6 us
    all_to_all x1, waiting for transfers between devices, local(): lax.all_to_all(stash, 'space', split_axis=1, concat_axis=0, tiled=True)  12.9 us
  transfers between devices with their start and end apart: 14, of which 12 were waited for; matrix products, arithmetic and copies ran while one was open for 18% of the time, Pallas kernels for 0%

commit v1 on v0

--- a/solution.py
+++ b/solution.py
@@ -170,17 +170,20 @@
     bias_sum = jnp.sum(grad_hidden, axis=0)
     out_sum = jnp.sum(cotangent, axis=(0, 1, 2), dtype=jnp.float32)
     totals = lax.psum(
-        (
-            grad_gain_one,
-            grad_gain_two,
-            pulled[2],
-            pulled[3],
-            pulled[4],
-            pulled[5],
-            bias_sum,
-            out_sum,
+        lax.psum(
+            (
+                grad_gain_one,
+                grad_gain_two,
+                pulled[2],
+                pulled[3],
+                pulled[4],
+                pulled[5],
+                bias_sum,
+                out_sum,
+            ),
+            "dp",
         ),
-        ("dp", "space"),
+        "space",
     )
     paired = (
         lax.psum_scatter(term_one, "dp", scatter_dimension=1, tiled=True),

time: 549 us -> 759 us (1.38)
  waiting for transfers between devices: 294 us -> 473 us
  blocking collectives: 41.9 us -> 66.1 us
    unnamed x7 -> x8, waiting for transfers between devices: 32.1 us -> 128 us
    reduce_scatter x1, waiting for transfers between devices: 33.6 us -> 113 us  [local(): lax.psum_scatter(term_one, 'dp', scatter_dimension=1, tiled=True)]
    psum x0 -> x1, blocking collectives: none -> 59.1 us  [local(): lax.psum(lax.psum((grad_gain_one, grad_gain_two, pulled[2], pulled[3], pu...]
    psum x1, blocking collectives: 41.9 us -> 7.01 us  [local(): lax.psum((grad_gain_one, grad_gain_two, pulled[2], pulled[3], pulled[4],...]
    all_to_all x1, waiting for transfers between devices: 0.01 us -> 13.1 us  [local(): lax.all_to_all(grad_merid_real, 'space', split_axis=1, concat_axis=2, til...]
    psum x1, waiting for transfers between devices: 43.3 us -> 32.7 us  [local(): lax.psum((grad_gain_one, grad_gain_two, pulled[2], pulled[3], pulled[4],...]
    unnamed x69 -> x85, local copies, waits for them, and re-layouts: 19.4 us -> 21 us
  transfers between devices with their start and end apart: 14 -> 15, of which waited for: 12 -> 14; matrix products, arithmetic and copies ran while one was open for 18% -> 10% of each run, Pallas kernels for 0% -> 0%
where the time goes in v1:
time: 759 us; the launch traced here: 751 us
  waiting for transfers between devices  473 us (62%)
  matrix products  93.1 us (12%)
  blocking collectives  66.1 us (9%)
  local copies, waits for them, and re-layouts  45.9 us (6%)
  starting transfers between devices  41.7 us (5%)
  other arithmetic  16 us (2%)
  between operations  15.6 us (2%)
    unnamed x8, waiting for transfers between devices  128 us
    reduce_scatter x1, waiting for transfers between devices, local(): lax.psum_scatter(term_one, 'dp', scatter_dimension=1, tiled=True)  113 us
    reduce_scatter x1, waiting for transfers between devices, local(): lax.psum_scatter(term_two, 'dp', scatter_dimension=1, tiled=True)  107 us
    psum x1, blocking collectives, local(): lax.psum(lax.psum((grad_gain_one, grad_gain_two, pulled[2], pulled[3], pu...  59.1 us
    psum x1, waiting for transfers between devices, local(): lax.psum((grad_gain_one, grad_gain_two, pulled[2], pulled[3], pulled[4],...  32.7 us
    unnamed x85, local copies, waits for them, and re-layouts  21 us
    dot_general x16, matrix products, meridian_apply(): return jnp.einsum('hk,bhmd->bkmd', table, field, precision=highest)  15.4 us
  transfers between devices with their start and end apart: 15, of which 14 were waited for; matrix products, arithmetic and copies ran while one was open for 10% of the time, Pallas kernels for 0%

profile of v1, /device:TPU:0, one launch (start us, length us, event | category | flops | bytes accessed | tf_op | source)
XLA Modules:
  0.0 751.2 jit_solution(2264385408436756193)
XLA Ops:
  7.2 7.4 all-to-all-start
  14.6 1.9 sort.17
  16.5 12.9 %all-to-all-done = bf16[1,16,2,8640]{3,2,0,1:T(2,128)(2,1)S(1)} async-done(((bf16[1,16,2,8640]{3,2,0,1:T(2,128)(2,1)}), bf16[1,16,2,8640]{3,2,0,1:T(2,128)(2,1)S(1)}, u32[]{:S(2)}, u32[]{:S(2)}) %all-to-all-start) | async-done | bytes 552992 | tf_op jit(solution)/shard_map/all_to_all | solution.py:102
  29.4 1.7 gather_fusion
  34.1 1.2 convolution_bitcast_fusion.4
  36.4 4.3 all-to-all-start.1
  40.8 1.3 fusion.29
  43.1 9.8 %all-to-all-done.1 = f32[2,1,64,768]{3,0,1,2:T(2,128)S(1)} async-done(((f32[2,1,64,768]{3,0,1,2:T(2,128)}), f32[2,1,64,768]{3,0,1,2:T(2,128)S(1)}, u32[]{:S(2)}, u32[]{:S(2)}) %all-to-all-start.1) | async-done | bytes 393248 | tf_op jit(solution)/shard_map/all_to_all | solution.py:116
  52.9 3.8 all-to-all-start.2
  57.1 1.3 fusion.143
  58.4 10.4 %all-to-all-done.2 = f32[2,1,64,768]{3,0,1,2:T(2,128)S(1)} async-done(((f32[2,1,64,768]{3,0,1,2:T(2,128)}), f32[2,1,64,768]{3,0,1,2:T(2,128)S(1)}, u32[]{:S(2)}, u32[]{:S(2)}) %all-to-all-start.2) | async-done | bytes 393248 | tf_op jit(solution)/shard_map/all_to_all | solution.py:117
  68.8 1.3 fusion.139
  70.1 1.7 fusion.28
  72.8 1.5 fusion.106
  74.2 1.3 fusion.27
  75.6 1.3 reshape.375
  79.0 1.6 fusion.111
  83.2 1.8 fusion.19
  87.6 3.6 all-to-all-start.3
  94.2 9.1 %all-to-all-done.3 = f32[2,16,4,768]{3,2,0,1:T(4,128)S(1)} async-done(((f32[2,16,4,768]{3,2,0,1:T(4,128)}), f32[2,16,4,768]{3,2,0,1:T(4,128)S(1)}, u32[]{:S(2)}, u32[]{:S(2)}) %all-to-all-start.3) | async-done | bytes 393248 | tf_op jit(solution)/shard_map/all_to_all | solution.py:125
  103.3 4.0 all-to-all-start.4
  107.3 6.4 fusion.368
  113.9 1.3 fusion.131
  115.3 4.2 all-to-all-done.4
  119.7 1.6 fusion.365
  122.7 9.5 %fusion.363 = (f32[3072]{0:T(1024)S(1)}, bf16[360,3072]{1,0:T(8,128)(2,1)S(1)}, f32[360,3072]{1,0:T(8,128)}) fusion(f32[360,3072]{1,0:T(8,128)} %fusion.368, f32[3072]{0:T(1024)S(1)} %copy-done.38, bf16[360,768]{1,0:T(8,128)(2,1)S(1)} %reshape.380, bf16[768,3072]{1,0:T(8,128)(2,1)} %param.20), kind=kOutput, calls=%fused_computation.455 | convolution fusion | flops 1723020288 | bytes 16355328 | tf_op jit(solution)/shard_map/dot_general | solution.py:132
  132.2 1.3 copy-done.20
  133.5 5.2 fusion.34
  138.8 1.4 reshape.381
  142.2 1.7 convert_reduce_fusion
  146.1 3.6 all-to-all-start.5
  151.8 10.0 %all-to-all-done.5 = f32[2,1,64,768]{3,0,1,2:T(2,128)S(1)} async-done(((f32[2,1,64,768]{3,0,1,2:T(2,128)}), f32[2,1,64,768]{3,0,1,2:T(2,128)S(1)}, u32[]{:S(2)}, u32[]{:S(2)}) %all-to-all-start.5) | async-done | bytes 393248 | tf_op jit(solution)/shard_map/all_to_all | solution.py:152
  161.8 3.6 all-to-all-start.6
  165.6 1.3 fusion.137
  166.9 10.6 %all-to-all-done.6 = f32[2,1,64,768]{3,0,1,2:T(2,128)S(1)} async-done(((f32[2,1,64,768]{3,0,1,2:T(2,128)}), f32[2,1,64,768]{3,0,1,2:T(2,128)S(1)}, u32[]{:S(2)}, u32[]{:S(2)}) %all-to-all-start.6) | async-done | bytes 393248 | tf_op jit(solution)/shard_map/all_to_all | solution.py:151
  177.5 1.3 fusion.133
  178.8 1.6 fusion.367
  180.7 2.8 fusion.85
  183.5 1.6 fusion.87
  185.2 1.3 fusion.366
  186.5 2.0 reshape.384
  188.6 2.5 fusion.61
  197.7 1.2 convolution_bitcast_fusion.10
  202.4 1.4 pad_add_fusion
  204.8 6.7 fusion.32
  212.6 8.9 %convolution_bitcast_fusion = f32[768,3072]{0,1:T(8,128)} fusion(bf16[360,768]{1,0:T(8,128)(2,1)S(1)} %copy-done.32, f32[360,3072]{1,0:T(8,128)} %get-tuple-element.91), kind=kOutput, calls=%fused_computation.3 | convolution fusion | flops 1708646400 | bytes 14413824 | tf_op jit(solution)/shard_map/td,tf->df/dot_general | solution.py:145
  221.5 32.7 %all-reduce.21.cloned.1.call-done = (f32[2,8,96,96]{3,2,1,0:T(8,128)}, f32[2,8,96,96]{3,2,1,0:T(8,128)}) async-done(((f32[2,8,96,96]{3,2,1,0:T(8,128)}, f32[2,8,96,96]{3,2,1,0:T(8,128)}), (f32[2,8,96,96]{3,2,1,0:T(8,128)}, f32[2,8,96,96]{3,2,1,0:T(8,128)})) %all-reduce.21.cloned.1.call-update) | async-done | bytes 1179664 | tf_op jit(solution)/shard_map/psum | solution.py:173
  254.3 112.9 %reduce-scatter.9.cloned.1.call-done = f32[768,1536]{1,0:T(8,128)} async-done(((f32[768,3072]{1,0:T(8,128)}), f32[768,1536]{1,0:T(8,128)}) %reduce-scatter.9.cloned.1.call-update) | async-done | bytes 4718608 | tf_op jit(solution)/shard_map/reduce_scatter | solution.py:189
  367.2 6.1 copy.208
  373.6 106.6 %reduce-scatter.11.cloned.1.call-done = f32[768,1536]{0,1:T(8,128)} async-done(((f32[768,3072]{0,1:T(8,128)}), f32[768,1536]{0,1:T(8,128)}) %reduce-scatter.11.cloned.1.call-update) | async-done | bytes 4718608 | tf_op jit(solution)/shard_map/reduce_scatter | solution.py:190
  481.3 1.9 fusion.124
  486.5 1.9 fusion.118
  493.6 5.6 all-to-all-start.8
  501.3 12.9 %all-to-all-done.8 = f32[2,16,4,768]{3,2,0,1:T(4,128)S(1)} async-done(((f32[2,16,4,768]{3,2,0,1:T(4,128)}), f32[2,16,4,768]{3,2,0,1:T(4,128)S(1)}, u32[]{:S(2)}, u32[]{:S(2)}) %all-to-all-start.8) | async-done | bytes 393248 | tf_op jit(solution)/shard_map/all_to_all | solution.py:161
  514.2 5.2 all-to-all-start.7
  519.8 13.1 %all-to-all-done.7 = f32[2,16,4,768]{3,2,0,1:T(4,128)S(1)} async-done(((f32[2,16,4,768]{3,2,0,1:T(4,128)}), f32[2,16,4,768]{3,2,0,1:T(4,128)S(1)}, u32[]{:S(2)}, u32[]{:S(2)}) %all-to-all-start.7) | async-done | bytes 393248 | tf_op jit(solution)/shard_map/all_to_all | solution.py:160
  533.1 1.3 convolution_bitcast_fusion.1
  534.5 1.7 multiply_reduce_fusion.2
  537.2 2.1 copy.188
  539.3 7.0 all-reduce.14
  546.3 59.1 %all-reduce.12 = (f32[3072]{0:T(1024)S(1)}, f32[768]{0:T(1024)S(1)}, f32[768]{0:T(1024)S(1)}, f32[768]{0:T(1024)S(1)}, f32[2,768]{1,0:T(2,128)S(1)}, /*index=5*/f32[2,768]{1,0:T(2,128)S(1)}) all-reduce(f32[3072]{0:T(1024)S(1)} %get-tuple-element.73, f32[768]{0:T(1024)S(1)} %get-tuple-element.74, ...), channel_id=1, replica_groups=mesh['dp'=2,'space'=16] {'space'}, use_global_device_ids=true, to_apply=%region_15.16 | all-reduce | flops 8448 | bytes 67584 | tf_op jit(solution)/shard_map/psum | solution.py:172
  609.0 2.2 broadcast_multiply_fusion.1
  612.1 51.2 %reduce-scatter.13.cloned.1.call-done = f32[96,768]{1,0:T(8,128)} async-done(((f32[1536,768]{1,0:T(8,128)}), f32[96,768]{1,0:T(8,128)}) %reduce-scatter.13.cloned.1.call-update) | async-done | bytes 294928
  665.3 76.5 %reduce-scatter.15.cloned.1.call-done = f32[96,768]{1,0:T(8,128)} async-done(((f32[1536,768]{1,0:T(8,128)}), f32[96,768]{1,0:T(8,128)}) %reduce-scatter.15.cloned.1.call-update) | async-done | bytes 294928
  (191 shorter events, 59.4 us)
Async XLA Ops:
  7.2 22.2 %all-to-all-start = ((bf16[1,16,2,8640]{3,2,0,1:T(2,128)(2,1)}), bf16[1,16,2,8640]{3,2,0,1:T(2,128)(2,1)S(1)}, u32[]{:S(2)}, u32[]{:S(2)}) async-start(bf16[1,16,2,8640]{3,2,0,1:T(2,128)(2,1)} %bitcast.441), calls=%async_computation | async-start | bytes 1114112 | tf_op jit(solution)/shard_map/all_to_all | solution.py:102
  33.4 0.7 copy-start.34
  36.4 16.5 %all-to-all-start.1 = ((f32[2,1,64,768]{3,0,1,2:T(2,128)}), f32[2,1,64,768]{3,0,1,2:T(2,128)S(1)}, u32[]{:S(2)}, u32[]{:S(2)}) async-start(f32[2,1,64,768]{3,0,1,2:T(2,128)} %copy.140), calls=%async_computation.1 | async-start | bytes 786432 | tf_op jit(solution)/shard_map/all_to_all | solution.py:116
  42.0 14.7 %copy-start.36 = (f32[2,768]{1,0:T(2,128)S(1)}, f32[2,768]{1,0:T(2,128)}, u32[]{:S(2)}) copy-start(f32[2,768]{1,0:T(2,128)} %param.16) | copy-start | bytes 18436
  42.0 14.9 %copy-start.37 = (f32[2,768]{1,0:T(2,128)S(1)}, f32[2,768]{1,0:T(2,128)}, u32[]{:S(2)}) copy-start(f32[2,768]{1,0:T(2,128)} %param.18) | copy-start | bytes 18436
  52.9 15.9 %all-to-all-start.2 = ((f32[2,1,64,768]{3,0,1,2:T(2,128)}), f32[2,1,64,768]{3,0,1,2:T(2,128)S(1)}, u32[]{:S(2)}, u32[]{:S(2)}) async-start(f32[2,1,64,768]{3,0,1,2:T(2,128)} %copy.142), calls=%async_computation.2 | async-start | bytes 786432 | tf_op jit(solution)/shard_map/all_to_all | solution.py:117
  70.1 1.9 copy-start.5
  72.1 2.1 copy-start.1
  72.1 2.1 copy-start.29
  75.6 1.3 copy-start.27
  76.9 3.7 copy-start.3
  76.9 1.3 copy-start.16
  78.2 2.4 copy-start.25
  81.3 1.3 copy-start.7
  82.1 1.1 copy-start.17
  86.1 5.1 copy-start.21
  87.6 15.7 %all-to-all-start.3 = ((f32[2,16,4,768]{3,2,0,1:T(4,128)}), f32[2,16,4,768]{3,2,0,1:T(4,128)S(1)}, u32[]{:S(2)}, u32[]{:S(2)}) async-start(f32[2,16,4,768]{3,2,0,1:T(4,128)} %copy.152), calls=%async_computation.3 | async-start | bytes 786432 | tf_op jit(solution)/shard_map/all_to_all | solution.py:125
  93.2 14.1 %copy-start.31 = (bf16[360,768]{1,0:T(8,128)(2,1)S(1)}, bf16[360,768]{1,0:T(8,128)(2,1)}, u32[]{:S(2)}) copy-start(bf16[360,768]{1,0:T(8,128)(2,1)} %reshape.373) | copy-start | bytes 1658884
  103.3 16.1 %all-to-all-start.4 = ((f32[2,16,4,768]{3,2,0,1:T(4,128)}), f32[2,16,4,768]{3,2,0,1:T(4,128)S(1)}, u32[]{:S(2)}, u32[]{:S(2)}) async-start(f32[2,16,4,768]{3,2,0,1:T(4,128)} %copy.155), calls=%async_computation.4 | async-start | bytes 786432 | tf_op jit(solution)/shard_map/all_to_all | solution.py:126
  121.3 0.7 copy-start.35
  122.0 0.7 copy-start.38
  122.7 9.5 %copy-start.23 = (bf16[360,768]{1,0:T(8,128)(2,1)}, bf16[360,768]{1,0:T(8,128)(2,1)S(1)}, u32[]{:S(2)}) copy-start(bf16[360,768]{1,0:T(8,128)(2,1)S(1)} %reshape.380) | copy-start | bytes 1658884
  132.2 1.3 copy-start.20
  140.1 1.0 copy-start
  141.2 1.1 copy-start.22
  146.1 15.7 %all-to-all-start.5 = ((f32[2,1,64,768]{3,0,1,2:T(2,128)}), f32[2,1,64,768]{3,0,1,2:T(2,128)S(1)}, u32[]{:S(2)}, u32[]{:S(2)}) async-start(f32[2,1,64,768]{3,0,1,2:T(2,128)} %copy.158), calls=%async_computation.5 | async-start | bytes 786432 | tf_op jit(solution)/shard_map/all_to_all | solution.py:152
  161.8 17.0 %copy-start.14 = (f32[2,1,64,768]{3,0,1,2:T(2,128)}, f32[2,1,64,768]{3,0,1,2:T(2,128)S(1)}, u32[]{:S(2)}) copy-start(f32[2,1,64,768]{3,0,1,2:T(2,128)S(1)} %all-to-all-done.5) | copy-start | bytes 1179652
  161.8 15.7 %all-to-all-start.6 = ((f32[2,1,64,768]{3,0,1,2:T(2,128)}), f32[2,1,64,768]{3,0,1,2:T(2,128)S(1)}, u32[]{:S(2)}, u32[]{:S(2)}) async-start(f32[2,1,64,768]{3,0,1,2:T(2,128)} %copy.160), calls=%async_computation.6 | async-start | bytes 786432 | tf_op jit(solution)/shard_map/all_to_all | solution.py:151
  165.3 88.9 %all-reduce.21.cloned.1.call-start = ((), (), s32[]{:S(2)}) async-start(), calls=%async_computation.18 | async-start | bytes 3145728 | tf_op jit(solution)/shard_map/psum | solution.py:173
  180.7 2.9 copy-start.18
  180.7 4.5 copy-start.15
  180.7 4.5 copy-start.28
  185.2 3.4 copy-start.8
  191.1 4.4 copy-start.9
  191.1 1.2 copy-start.13
  192.3 2.1 copy-start.2
  193.4 2.1 copy-start.4
  194.4 2.1 copy-start.19
  194.4 2.1 copy-start.26
  194.4 2.1 copy-start.33
  197.6 2.3 copy-start.10
  203.8 1.1 copy-start.24
  203.8 163.4 %reduce-scatter.9.cloned.1.call-start = ((), (), s32[]{:S(2)}) async-start(), calls=%async_computation.13 | async-start | bytes 14155776 | tf_op jit(solution)/shard_map/reduce_scatter | solution.py:189
  211.5 1.1 copy-start.32
  211.5 268.6 %reduce-scatter.11.cloned.1.call-start = ((), (), s32[]{:S(2)}) async-start(), calls=%async_computation.14 | async-start | bytes 14155776 | tf_op jit(solution)/shard_map/reduce_scatter | solution.py:190
  221.5 387.5 %all-reduce.19.cloned.1.call-start = ((), (), s32[]{:S(2)}) async-start(), calls=%async_computation.17 | async-start | bytes 3145728 | tf_op jit(solution)/shard_map/psum | solution.py:172
  254.3 409.0 %reduce-scatter.13.cloned.1.call-start = ((), (), s32[]{:S(2)}) async-start(), calls=%async_computation.15 | async-start | bytes 5013504
  373.3 368.5 %reduce-scatter.15.cloned.1.call-start = ((), (), s32[]{:S(2)}) async-start(), calls=%async_computation.16 | async-start | bytes 5013504
  480.2 1.1 copy-start.6
  481.3 1.9 copy-start.11
  486.5 1.9 copy-start.12
  493.6 20.6 %all-to-all-start.8 = ((f32[2,16,4,768]{3,2,0,1:T(4,128)}), f32[2,16,4,768]{3,2,0,1:T(4,128)S(1)}, u32[]{:S(2)}, u32[]{:S(2)}) async-start(f32[2,16,4,768]{3,2,0,1:T(4,128)} %copy.176), calls=%async_computation.8 | async-start | bytes 786432 | tf_op jit(solution)/shard_map/all_to_all | solution.py:161
  514.2 18.7 %all-to-all-start.7 = ((f32[2,16,4,768]{3,2,0,1:T(4,128)}), f32[2,16,4,768]{3,2,0,1:T(4,128)S(1)}, u32[]{:S(2)}, u32[]{:S(2)}) async-start(f32[2,16,4,768]{3,2,0,1:T(4,128)} %copy.173), calls=%async_computation.7 | async-start | bytes 786432 | tf_op jit(solution)/shard_map/all_to_all | solution.py:160
  609.0 2.2 copy-start.30
Sparse Core Ops, SparseCore 0:
  203.9 50.2 all-reduce.20
  256.5 110.6 reduce-scatter.8
  369.5 110.6 reduce-scatter.10
  483.6 101.3 all-reduce.18
  588.7 74.5 reduce-scatter.12
  667.0 74.7 reduce-scatter.14
